TPU v7x, 32 devices: a whole 2x2x4 slice. The times are simulated.
32 devices in a mesh: ep: 8 (over z, y), tp: 4 (over x, core).
Axes of the slice: x: 2, y: 2, z: 4, core: 2. Of those that a mesh axis runs over, the one named last changes fastest.
Arguments:
- hidden_in: bfloat16 [4096, 1536], P(('ep', 'tp')), may hold values from -6 to 6
- gain_attn: bfloat16 [1536], replicated, may hold values from 0.5 to 1.5
- w_query: bfloat16 [1536, 1536], P('tp'), may hold values from -0.15625 to 0.15625
- key_projection_weight: bfloat16 [512, 1536], P('tp'), may hold values from -0.15625 to 0.15625
- value_projection_weight: bfloat16 [512, 1536], P('tp'), may hold values from -0.15625 to 0.15625
- w_out: bfloat16 [1536, 1536], P('tp'), may hold values from -0.625 to 0.625
- gain_ffn: bfloat16 [1536], replicated, may hold values from 0.5 to 1.5
- w_router: bfloat16 [16, 1536], replicated, may hold values from -0.078125 to 0.078125
- w_gate: bfloat16 [16, 1536, 512], P('ep', None, 'tp'), may hold values from -0.15625 to 0.15625
- w_up: bfloat16 [16, 1536, 512], P('ep', None, 'tp'), may hold values from -0.15625 to 0.15625
- w_down: bfloat16 [16, 512, 1536], P('ep', 'tp'), may hold values from -0.75 to 0.75
- expert_ids: int32 [4096, 8], P('ep'), may hold values from 0 to 15, all different within a row; in each aligned block of 512 rows (0 to 511, 512 to 1023, ...) at most 512 rows name the same one
- slot_order: int32 [4096, 8], P('ep'), may hold values from 0 to 4095, as said below
- segment: int32 [4096], P('ep'), may hold values from 0 to 12, as said below
- position: int32 [4096], P('ep'), may hold values from 0 to 303, as said below
- cotangent: bfloat16 [4096, 1536], P(('ep', 'tp')), may hold values from -6 to 6
Outputs:
- output: bfloat16 [4096, 1536], P(('ep', 'tp'))
- grad_input: float32 [4096, 1536], P(('ep', 'tp'))
- grad_gain_attn: float32 [1536], replicated
- grad_query: float32 [1536, 1536], P('tp')
- grad_key: float32 [512, 1536], P('tp')
- grad_value: float32 [512, 1536], P('tp')
- grad_out: float32 [1536, 1536], P('tp')
- grad_gain_ffn: float32 [1536], replicated
- grad_router: float32 [16, 1536], replicated
- grad_gate: float32 [16, 1536, 512], P('ep', None, 'tp')
- grad_up: float32 [16, 1536, 512], P('ep', None, 'tp')
- grad_down: float32 [16, 512, 1536], P('ep', 'tp')
Inputs may be any that keep to these rules, and one draw needn't show every extreme that they name: `expert_ids`: in the 512 rows of one index of ep no expert is named by more than 512 rows, a bound that some block reaches of them. `slot_order`: within the 512 rows of one index of ep every number from 0 to 4095 appears once. Each tree is 512 consecutive tokens: its first 256 tokens are segment 0; segments 1 to 4 (branches, parent 0) hold 32 tokens each and segments 5 to 12 (leaves, parent 1 + (s - 5) // 2) hold 16 tokens each, each segment contiguous, in an order drawn for every tree. A token's position is its depth on its path: trunk 0 to 255, a branch from 256, a leaf from 288, rising by one along its segment.
All inputs are finite; a program needn't handle non-finite values.
Results may differ from a plain program's by a relative error of at most 0.02.
Values may be sent and summed in bfloat16 or wider, within the bound.
A program may use at most 320 MiB of HBM per device.

v0:
```python
import jax
import jax.numpy as jnp
from jax import lax
from jax.sharding import PartitionSpec as P

HEAD_DIMENSION = 64
TREE_TOKENS = 512
CAP = 2304
EPSILON = 1e-06
ROPE_BASE = 10000.0
EXACT_PRECISION = lax.Precision.HIGHEST


def rope_tables(position, head_width):
    half_width = head_width // 2
    freqs = ROPE_BASE ** (-(jnp.arange(half_width, dtype=jnp.float32) * 2.0 / head_width))
    angle = position.astype(jnp.float32)[:, None] * freqs[None, :]
    return (jnp.cos(angle)[:, None, :], jnp.sin(angle)[:, None, :])


def apply_rotation(value_rows, cosine_lookup, sine_lookup):
    half_width = value_rows.shape[-1] // 2
    first = value_rows[..., :half_width]
    second = value_rows[..., half_width:]
    return jnp.concatenate(
        [
            first * cosine_lookup - second * sine_lookup,
            first * sine_lookup + second * cosine_lookup,
        ],
        axis=-1,
    )


def rotate_back(grads, cosine_lookup, sine_lookup):
    half_width = grads.shape[-1] // 2
    first = grads[..., :half_width]
    second = grads[..., half_width:]
    return jnp.concatenate(
        [
            first * cosine_lookup + second * sine_lookup,
            second * cosine_lookup - first * sine_lookup,
        ],
        axis=-1,
    )


def norm_scale(value_rows):
    return lax.rsqrt(jnp.mean(value_rows * value_rows, axis=-1, keepdims=True) + EPSILON)


def norm_back(value_rows, scale, gain, grad_normed):
    weighted = grad_normed * gain
    inner = jnp.mean(value_rows * weighted, axis=-1, keepdims=True)
    grad_values = scale * weighted - value_rows * (scale * scale * scale) * inner
    return (grad_values, jnp.sum(grad_normed * value_rows * scale, axis=0))


def group_rows(value_rows):
    return lax.all_gather(value_rows, "tp", axis=0, tiled=True)


def group_totals(value_rows):
    return lax.psum_scatter(value_rows, "tp", scatter_dimension=0, tiled=True)


def gather_all(value_rows):
    return lax.all_gather(value_rows, ("ep", "tp"), axis=0, tiled=True)


def total_all(value_rows):
    return lax.psum_scatter(value_rows, ("ep", "tp"), scatter_dimension=0, tiled=True)


def kept_pairs(expert_ids, slot_order, expert_count, row_start, share):
    experts = jnp.arange(expert_count, dtype=jnp.int32)
    chosen = expert_ids[:, :, None] == experts[None, None, :]
    last = jnp.int32(1 << 30)
    order = jnp.min(jnp.where(chosen, slot_order[:, :, None], last), axis=1)
    counts = jnp.sum((order < last).astype(jnp.int32), axis=0)
    every = lax.all_gather(counts, "ep")
    earlier = jnp.arange(every.shape[0], dtype=jnp.int32) < lax.axis_index("ep")
    offsets = jnp.sum(jnp.where(earlier[:, None], every, 0), axis=0)
    own = lax.dynamic_slice_in_dim(order, row_start, share, 0)
    rank = jnp.sum((order[:, None, :] < own[None, :, :]).astype(jnp.int32), axis=0)
    used = own < last
    return (used, used & (rank + offsets[None, :] < CAP))


def visible_block(query_seg, query_pos, query_row, key_seg, key_pos, key_row):
    seg_q = query_seg[:, None]
    seg_k = key_seg[None, :]
    above = (
        (seg_k == seg_q)
        | (seg_k == 0)
        | (seg_k >= 1) & (seg_k <= 4) & (seg_q >= 5) & ((seg_q - 5) // 2 + 1 == seg_k)
    )
    same_tree = query_row[:, None] // TREE_TOKENS == key_row[None, :] // TREE_TOKENS
    return above & same_tree & (key_pos[None, :] <= query_pos[:, None])


def block_scores(query_part, key_rows, allowed, scale):
    scores = (
        jnp.einsum("qkgd,pkd->kgqp", query_part, key_rows, preferred_element_type=jnp.float32)
        * scale
    )
    return jnp.where(allowed[None, None], scores, -1e30)


def attend_forward(query_rows, key_rows, value_rows, segment, position):
    total_rows = query_rows.shape[0]
    scale = query_rows.shape[-1] ** (-0.5)
    row_ids = jnp.arange(total_rows, dtype=jnp.int32)
    allowed = visible_block(segment, position, row_ids, segment, position, row_ids)
    scores = block_scores(query_rows, key_rows, allowed, scale)
    top_score = jnp.max(scores, axis=-1, keepdims=True)
    weights = jnp.exp(scores - top_score)
    weight_sum = jnp.sum(weights, axis=-1, keepdims=True)
    probs = (weights / weight_sum).astype(jnp.bfloat16)
    outputs = jnp.einsum(
        "kgqp,pkd->qkgd", probs, value_rows, preferred_element_type=jnp.float32
    ).astype(jnp.bfloat16)
    log_sums = [top_score + jnp.log(weight_sum)]
    return (outputs, log_sums)


def attend_backward(
    query_rows, key_rows, value_rows, segment, position, log_sums, grad_heads, block_rows
):
    total_rows = query_rows.shape[0]
    scale = query_rows.shape[-1] ** (-0.5)
    row_ids = jnp.arange(total_rows, dtype=jnp.int32)
    grad_keys = jnp.zeros(key_rows.shape, jnp.float32)
    grad_values = jnp.zeros(value_rows.shape, jnp.float32)
    grad_query = []
    for number, first_row in enumerate(range(0, total_rows, block_rows)):
        allowed = visible_block(segment, position, row_ids, segment, position, row_ids)
        scores = block_scores(query_rows, key_rows, allowed, scale)
        probs = jnp.where(allowed[None, None], jnp.exp(scores - log_sums[number]), 0.0)
        grad_values = jnp.einsum(
            "kgqp,qkgd->pkd",
            probs.astype(jnp.bfloat16),
            grad_heads,
            preferred_element_type=jnp.float32,
        )
        grad_probs = jnp.einsum(
            "qkgd,pkd->kgqp", grad_heads, value_rows, preferred_element_type=jnp.float32
        )
        inner = jnp.sum(probs * grad_probs, axis=-1, keepdims=True)
        grad_scores = (probs * (grad_probs - inner)).astype(jnp.bfloat16)
        grad_query.append(
            jnp.einsum("kgqp,pkd->qkgd", grad_scores, key_rows, preferred_element_type=jnp.float32)
            * scale
        )
        grad_keys = (
            jnp.einsum(
                "kgqp,qkgd->pkd", grad_scores, query_rows, preferred_element_type=jnp.float32
            )
            * scale
        )
    return (grad_query[0], grad_keys, grad_values)


def local(
    hidden_in,
    gain_attn,
    w_query,
    key_projection_weight,
    value_projection_weight,
    w_out,
    gain_ffn,
    w_router,
    w_gate,
    w_up,
    w_down,
    expert_ids,
    slot_order,
    segment,
    position,
    cotangent,
):
    model_width = w_query.shape[1]
    head_width = HEAD_DIMENSION
    local_heads = w_query.shape[0] // head_width
    local_kv = key_projection_weight.shape[0] // head_width
    group_factor = local_heads // local_kv
    token_count = expert_ids.shape[0]
    share = hidden_in.shape[0]
    row_start = lax.axis_index("tp") * share
    expert_count = w_router.shape[0]
    per_owner = w_gate.shape[0]
    block_rows = 512
    used, kept = kept_pairs(expert_ids, slot_order, expert_count, row_start, share)
    cot_all = gather_all(cotangent)
    inputs_own = hidden_in.astype(jnp.float32)
    gain_one = gain_attn.astype(jnp.float32)
    gain_two = gain_ffn.astype(jnp.float32)
    scale_one = norm_scale(inputs_own)
    first_normalized = group_rows((inputs_own * scale_one * gain_one).astype(jnp.bfloat16))
    cosine_lookup, sine_lookup = rope_tables(position, head_width)
    query_proj = jnp.einsum(
        "rd,fd->rf", first_normalized, w_query, preferred_element_type=jnp.float32
    ).reshape(token_count, local_heads, head_width)
    key_proj = jnp.einsum(
        "rd,fd->rf", first_normalized, key_projection_weight, preferred_element_type=jnp.float32
    ).reshape(token_count, local_kv, head_width)
    query_rows = (
        apply_rotation(query_proj, cosine_lookup, sine_lookup)
        .astype(jnp.bfloat16)
        .reshape(token_count, local_kv, group_factor, head_width)
    )
    key_rows = apply_rotation(key_proj, cosine_lookup, sine_lookup).astype(jnp.bfloat16)
    value_rows = (
        jnp.einsum(
            "rd,fd->rf",
            first_normalized,
            value_projection_weight,
            preferred_element_type=jnp.float32,
        )
        .astype(jnp.bfloat16)
        .reshape(token_count, local_kv, head_width)
    )
    head_outputs, log_sums = attend_forward(query_rows, key_rows, value_rows, segment, position)
    head_outputs = head_outputs.reshape(token_count, local_heads * head_width)
    middle_own = inputs_own + group_totals(
        jnp.dot(head_outputs, w_out, preferred_element_type=jnp.float32)
    )
    scale_two = norm_scale(middle_own)
    normed_own = (middle_own * scale_two * gain_two).astype(jnp.bfloat16)
    normed_two = gather_all(normed_own)
    logits = jnp.einsum("rd,ed->re", normed_own, w_router, preferred_element_type=jnp.float32)
    top_logit = jnp.max(jnp.where(used, logits, -jnp.inf), axis=-1, keepdims=True)
    powers = jnp.where(used, jnp.exp(logits - top_logit), 0.0)
    gates = powers / jnp.sum(powers, axis=-1, keepdims=True)
    first_expert = lax.axis_index("ep") * per_owner
    kept_all = lax.dynamic_slice_in_dim(
        gather_all(kept.astype(jnp.float32)), first_expert, per_owner, 1
    )
    gate_all = lax.dynamic_slice_in_dim(
        gather_all(jnp.where(kept, gates, 0.0)), first_expert, per_owner, 1
    )
    units = w_gate.shape[2]
    gate_in = jnp.concatenate([w_gate[e] for e in range(per_owner)], axis=1)
    up_in = jnp.concatenate([w_up[e] for e in range(per_owner)], axis=1)
    down_in = w_down.reshape(per_owner * units, model_width)
    spread = jnp.repeat(gate_all, units, axis=1)
    gate_act = jnp.dot(normed_two, gate_in, preferred_element_type=jnp.float32)
    up_act = jnp.dot(normed_two, up_in, preferred_element_type=jnp.float32)
    back_act = jnp.einsum("rd,fd->rf", cot_all, down_in, preferred_element_type=jnp.float32)
    sigma = jax.nn.sigmoid(gate_act)
    hidden = gate_act * sigma * up_act
    weighted_hidden = (spread * hidden).astype(jnp.bfloat16)
    grad_hidden = spread * back_act
    grad_gate_act = (grad_hidden * up_act * sigma * (1.0 + gate_act * (1.0 - sigma))).astype(
        jnp.bfloat16
    )
    grad_up_act = (grad_hidden * gate_act * sigma).astype(jnp.bfloat16)
    grad_gates_part = kept_all * jnp.sum((hidden * back_act).reshape(-1, per_owner, units), axis=2)
    grad_rows = (
        jnp.einsum("rf,df->rd", grad_gate_act, gate_in, preferred_element_type=jnp.float32)
        + jnp.einsum("rf,df->rd", grad_up_act, up_in, preferred_element_type=jnp.float32)
    ).astype(jnp.bfloat16)
    grad_normed_own = total_all(grad_rows).astype(jnp.float32)
    grad_gates_own = total_all(
        lax.dynamic_update_slice_in_dim(
            jnp.zeros((normed_two.shape[0], expert_count), jnp.float32),
            grad_gates_part,
            first_expert,
            1,
        )
    )
    combined = jnp.dot(weighted_hidden, down_in, preferred_element_type=jnp.float32).astype(
        jnp.bfloat16
    )
    output_own = (middle_own + total_all(combined).astype(jnp.float32)).astype(jnp.bfloat16)
    grad_w_gate = jnp.einsum(
        "rd,ref->edf",
        normed_two,
        grad_gate_act.reshape(-1, per_owner, units),
        preferred_element_type=jnp.float32,
    )
    grad_w_up = jnp.einsum(
        "rd,ref->edf",
        normed_two,
        grad_up_act.reshape(-1, per_owner, units),
        preferred_element_type=jnp.float32,
    )
    grad_w_down = jnp.einsum(
        "rf,rd->fd", weighted_hidden, cot_all, preferred_element_type=jnp.float32
    ).reshape(per_owner, units, model_width)
    inner_gate = jnp.sum(gates * grad_gates_own, axis=-1, keepdims=True)
    grad_logits = gates * (grad_gates_own - inner_gate)
    router_f = w_router.astype(jnp.float32)
    grad_normed_own = grad_normed_own + jnp.dot(grad_logits, router_f, precision=EXACT_PRECISION)
    grad_router = jnp.dot(grad_logits.T, normed_own.astype(jnp.float32), precision=EXACT_PRECISION)
    grad_middle_back, grad_gain_ffn = norm_back(middle_own, scale_two, gain_two, grad_normed_own)
    grad_middle = cotangent.astype(jnp.float32) + grad_middle_back
    grad_attn = group_rows(grad_middle.astype(jnp.bfloat16))
    grad_w_out = jnp.einsum(
        "rf,rd->fd", head_outputs, grad_attn, preferred_element_type=jnp.float32
    )
    grad_heads = (
        jnp.einsum("rd,fd->rf", grad_attn, w_out, preferred_element_type=jnp.float32)
        .astype(jnp.bfloat16)
        .reshape(token_count, local_kv, group_factor, head_width)
    )
    grad_query, grad_keys, grad_values = attend_backward(
        query_rows, key_rows, value_rows, segment, position, log_sums, grad_heads, block_rows
    )
    grad_query_proj = (
        rotate_back(
            grad_query.reshape(token_count, local_heads, head_width), cosine_lookup, sine_lookup
        )
        .astype(jnp.bfloat16)
        .reshape(token_count, local_heads * head_width)
    )
    grad_key_proj = (
        rotate_back(grad_keys, cosine_lookup, sine_lookup)
        .astype(jnp.bfloat16)
        .reshape(token_count, local_kv * head_width)
    )
    grad_value_proj = grad_values.astype(jnp.bfloat16).reshape(token_count, local_kv * head_width)
    grad_w_query = jnp.einsum(
        "rf,rd->fd", grad_query_proj, first_normalized, preferred_element_type=jnp.float32
    )
    grad_w_key = jnp.einsum(
        "rf,rd->fd", grad_key_proj, first_normalized, preferred_element_type=jnp.float32
    )
    grad_w_value = jnp.einsum(
        "rf,rd->fd", grad_value_proj, first_normalized, preferred_element_type=jnp.float32
    )
    grad_normed_one = jnp.einsum(
        "rf,fd->rd", grad_query_proj, w_query, preferred_element_type=jnp.float32
    )
    grad_normed_one = grad_normed_one + jnp.einsum(
        "rf,fd->rd", grad_key_proj, key_projection_weight, preferred_element_type=jnp.float32
    )
    grad_normed_one = grad_normed_one + jnp.einsum(
        "rf,fd->rd", grad_value_proj, value_projection_weight, preferred_element_type=jnp.float32
    )
    grad_one_own = group_totals(grad_normed_one)
    grad_inputs_back, grad_gain_attn = norm_back(inputs_own, scale_one, gain_one, grad_one_own)
    grad_input = grad_middle + grad_inputs_back
    grad_w_query, grad_w_key, grad_w_value, grad_w_out = (
        lax.psum(grad_w_query.astype(jnp.bfloat16), "ep").astype(jnp.float32),
        lax.psum(grad_w_key.astype(jnp.bfloat16), "ep").astype(jnp.float32),
        lax.psum(grad_w_value.astype(jnp.bfloat16), "ep").astype(jnp.float32),
        lax.psum(grad_w_out.astype(jnp.bfloat16), "ep").astype(jnp.float32),
    )
    grad_gain_attn, grad_gain_ffn, grad_router = lax.psum(
        (grad_gain_attn, grad_gain_ffn, grad_router), ("ep", "tp")
    )
    return (
        output_own,
        grad_input,
        grad_gain_attn,
        grad_w_query,
        grad_w_key,
        grad_w_value,
        grad_w_out,
        grad_gain_ffn,
        grad_router,
        grad_w_gate,
        grad_w_up,
        grad_w_down,
    )


def solution(mesh):
    placed = (
        P(("ep", "tp"), None),
        P(),
        P("tp", None),
        P("tp", None),
        P("tp", None),
        P("tp", None),
        P(),
        P(),
        P("ep", None, "tp"),
        P("ep", None, "tp"),
        P("ep", "tp", None),
        P("ep", None),
        P("ep", None),
        P("ep"),
        P("ep"),
        P(("ep", "tp"), None),
    )
    return jax.shard_map(
        local,
        mesh=mesh,
        in_specs=placed,
        out_specs=(
            P(("ep", "tp"), None),
            P(("ep", "tp"), None),
            P(),
            P("tp", None),
            P("tp", None),
            P("tp", None),
            P("tp", None),
            P(),
            P(),
            P("ep", None, "tp"),
            P("ep", None, "tp"),
            P("ep", "tp", None),
        ),
        check_vma=False,
    )
```

profile of v0, /device:TPU:8, one launch (start us, length us, event | category | flops | bytes accessed | tf_op | source)
XLA Modules:
  0.0 1170.9 jit_solution(3175409998038890623)
XLA Ops:
  7.3 1.3 fusion.29
  9.8 1.9 fusion.31
  14.2 1.6 compare_and_fusion
  15.8 16.9 %all-gather.6.cloned.1.call-done = bf16[512,1536]{1,0:T(8,128)(2,1)} async-done(((bf16[128,1536]{1,0:T(8,128)(2,1)}), bf16[512,1536]{1,0:T(8,128)(2,1)}) %all-gather.6.cloned.1.call-update) | async-done | bytes 1572880 | tf_op jit(solution)/shard_map/all_gather | solution.py:59
  32.7 2.1 fusion.66
  34.9 2.2 fusion.67
  39.5 1.7 copy-done.2
  44.2 2.6 fusion.68
  47.6 37.4 %reduce-scatter.6.cloned.1.call-done = f32[128,1536]{1,0:T(8,128)} async-done(((f32[512,1536]{1,0:T(8,128)}), f32[128,1536]{1,0:T(8,128)}) %reduce-scatter.6.cloned.1.call-update) | async-done | bytes 786448 | tf_op jit(solution)/shard_map/reduce_scatter | solution.py:63
  85.0 1.4 multiply_reduce_fusion.2
  89.1 1.4 select_reduce_fusion
  90.5 1.6 copy.39
  92.1 1.2 dynamic-slice
  94.0 1.4 convert_reduce_fusion.1
  95.9 1.3 dynamic-update-slice
  97.2 11.1 all-reduce
  108.2 1.3 reshape.451
  111.0 4.3 convert_reduce_fusion
  115.3 1.4 fusion.63
  116.7 36.5 %all_gather.30 = f32[4096,16]{0,1:T(8,128)} all-gather(f32[128,16]{0,1:T(8,128)S(1)} %get-tuple-element.48), channel_id=1, replica_groups=mesh['ep'=8,'tp'=4] {'ep','tp'}, dimensions={0}, use_global_device_ids=true | all-gather | bytes 270336 | tf_op jit(solution)/shard_map/all_gather | solution.py:67
  153.2 2.0 slice_bitcast_fusion.3
  155.2 2.0 slice_bitcast_fusion.1
  157.3 29.2 %all-gather.8.cloned.1.call-done = bf16[4096,1536]{1,0:T(8,128)(2,1)} async-done(((bf16[128,1536]{1,0:T(8,128)(2,1)}), bf16[4096,1536]{1,0:T(8,128)(2,1)}) %all-gather.8.cloned.1.call-update) | async-done | bytes 12582928 | tf_op jit(solution)/shard_map/all_gather | solution.py:67
  186.5 10.3 fusion.38
  196.8 10.2 fusion.40
  207.0 76.8 %all-gather.10.cloned.1.call-done = bf16[4096,1536]{1,0:T(8,128)(2,1)} async-done(((bf16[128,1536]{1,0:T(8,128)(2,1)}), bf16[4096,1536]{1,0:T(8,128)(2,1)}) %all-gather.10.cloned.1.call-update) | async-done | bytes 12582928 | tf_op jit(solution)/shard_map/all_gather | solution.py:67
  283.8 12.7 %bitcast_reduce_fusion = (f32[4096,2]{0,1:T(2,128)S(1)}, f32[4096,256]{0,1:T(8,128)}) fusion(f32[4096,256]{0,1:T(8,128)} %fusion.38, f32[4096,256]{0,1:T(8,128)} %fusion.40, bf16[4096,1536]{1,0:T(8,128)(2,1)} %all-gather.10.cloned.1.call-done, bf16[256,1536]{1,0:T(8,128)(2,1)} %bitcast.149), kind=kOutput, calls=%fused_computation.19 | convolution fusion | flops 3228557312 | bytes 25985024 | tf_op jit(solution)/shard_map/rd,fd->rf/dot_general | solution.py:248
  297.3 1.5 multiply_dynamic-update-slice_fusion
  301.9 110.8 %reduce-scatter.12.cloned.1.call-done = f32[128,16]{0,1:T(8,128)} async-done(((f32[4096,16]{0,1:T(8,128)}), f32[128,16]{0,1:T(8,128)}) %reduce-scatter.12.cloned.1.call-update) | async-done | bytes 8208 | tf_op jit(solution)/shard_map/reduce_scatter | solution.py:71
  412.7 1.2 multiply_reduce_fusion.3
  413.9 49.5 %all_gather.27 = f32[4096,16]{0,1:T(8,128)S(1)} all-gather(f32[128,16]{0,1:T(8,128)S(1)} %get-tuple-element.70), channel_id=1, replica_groups=mesh['ep'=8,'tp'=4] {'ep','tp'}, dimensions={0}, use_global_device_ids=true | all-gather | bytes 270336 | tf_op jit(solution)/shard_map/all_gather | solution.py:67
  463.5 7.3 multiply_convert_fusion
  470.8 10.4 fusion.39
  481.2 15.3 %add_convert_fusion = bf16[4096,1536]{1,0:T(8,128)(2,1)} fusion(f32[4096,1536]{1,0:T(8,128)} %fusion.39, bf16[4096,256]{0,1:T(8,128)(2,1)} %get-tuple-element.53, bf16[1536,128]{1,0:T(8,128)(2,1)} %get-tuple-element.64, bf16[1536,128]{1,0:T(8,128)(2,1)} %get-tuple-element.63), kind=kOutput, calls=%fused_computation | convolution fusion | flops 3235381248 | bytes 40632320 | tf_op jit(solution)/shard_map/rf,df->rd/dot_general | solution.py:260
  496.6 9.8 convolution_convert_fusion
  506.4 149.4 %reduce-scatter.10.cloned.1.call-done = bf16[128,1536]{1,0:T(8,128)(2,1)} async-done(((bf16[4096,1536]{1,0:T(8,128)(2,1)}), bf16[128,1536]{1,0:T(8,128)(2,1)}) %reduce-scatter.10.cloned.1.call-update) | async-done | bytes 393232 | tf_op jit(solution)/shard_map/reduce_scatter | solution.py:71
  655.7 3.2 multiply_reduce_fusion
  659.5 158.1 %reduce-scatter.8.cloned.1.call-done = bf16[128,1536]{1,0:T(8,128)(2,1)} async-done(((bf16[4096,1536]{1,0:T(8,128)(2,1)}), bf16[128,1536]{1,0:T(8,128)(2,1)}) %reduce-scatter.8.cloned.1.call-update) | async-done | bytes 393232 | tf_op jit(solution)/shard_map/reduce_scatter | solution.py:71
  817.6 2.9 fusion.62
  821.7 18.1 %all-gather.12.cloned.1.call-done = bf16[512,1536]{1,0:T(8,128)(2,1)} async-done(((bf16[128,1536]{1,0:T(8,128)(2,1)}), bf16[512,1536]{1,0:T(8,128)(2,1)}) %all-gather.12.cloned.1.call-update) | async-done | bytes 1572880 | tf_op jit(solution)/shard_map/all_gather | solution.py:59
  839.8 2.4 convolution_convert_fusion.5
  842.2 4.1 fusion.26
  846.4 4.5 fusion.4
  850.9 4.7 fusion.6
  858.2 1.8 convolution_convert_fusion.1
  862.2 1.8 convolution_convert_fusion.2
  864.2 2.3 fusion.69
  867.5 2.2 convolution_add_fusion
  870.0 7.2 fusion.17
  877.2 1.6 copy.44
  878.8 9.8 fusion.14
  888.7 3.1 copy.43
  892.7 9.8 fusion.70
  902.6 90.6 %all-reduce.8.cloned.1.call-done = (bf16[384,1536]{1,0:T(8,128)(2,1)}, bf16[128,1536]{1,0:T(8,128)(2,1)}, bf16[128,1536]{1,0:T(8,128)(2,1)}, bf16[384,1536]{1,0:T(8,128)(2,1)}) async-done(((bf16[384,1536]{1,0:T(8,128)(2,1)}, bf16[128,1536]{1,0:T(8,128)(2,1)}, bf16[128,1536]{1,0:T(8,128)(2,1)}, bf16[384,1536]{1,0:T(8,128)(2,1)}), (bf16[384,1536]{1,0:T(8,128)(2,1)}, bf16[128,1536]{1,0:T(8,128)(2,1)}, ...) | async-done | bytes 3145744 | tf_op jit(solution)/shard_map/psum | solution.py:344
  993.2 2.1 convert_element_type.156
  995.3 2.0 convert_element_type.158
  997.3 1.7 convert_element_type.154
  999.0 1.7 convert_element_type.160
  1000.7 33.4 %reduce-scatter.14.cloned.1.call-done = f32[128,1536]{1,0:T(8,128)} async-done(((f32[512,1536]{1,0:T(8,128)}), f32[128,1536]{1,0:T(8,128)}) %reduce-scatter.14.cloned.1.call-update) | async-done | bytes 786448 | tf_op jit(solution)/shard_map/reduce_scatter | solution.py:63
  1034.1 1.4 fusion.37
  1035.5 2.4 fusion.34
  1037.8 39.4 %all-reduce.1 = (f32[1536]{0:T(1024)}, f32[1536]{0:T(1024)}) all-reduce(f32[1536]{0:T(1024)S(1)} %get-tuple-element.38, f32[1536]{0:T(1024)S(1)} %copy-done.40), channel_id=1, replica_groups=mesh['ep'=8,'tp'=4] {'ep','tp'}, use_global_device_ids=true, to_apply=%region_21.22 | all-reduce | flops 3072 | bytes 24576 | tf_op jit(solution)/shard_map/psum | solution.py:349
  1077.3 85.3 %all-reduce.6.cloned.1.call-done = f32[16,1536]{1,0:T(8,128)} async-done(((f32[16,1536]{1,0:T(8,128)}), f32[16,1536]{1,0:T(8,128)}) %all-reduce.6.cloned.1.call-update) | async-done | bytes 98320 | tf_op jit(solution)/shard_map/psum | solution.py:349
  1162.6 1.5 copy.60
  (165 shorter events, 27.1 us)
Async XLA Ops:
  7.2 37.1 %copy-start = (bf16[384,1536]{1,0:T(8,128)(2,1)S(1)}, bf16[384,1536]{1,0:T(8,128)(2,1)}, u32[]{:S(2)}) copy-start(bf16[384,1536]{1,0:T(8,128)(2,1)} %param.21) | copy-start | bytes 3538948
  7.2 27.7 %copy-start.20 = (bf16[384,1536]{1,0:T(8,128)(2,1)S(1)}, bf16[384,1536]{1,0:T(8,128)(2,1)}, u32[]{:S(2)}) copy-start(bf16[384,1536]{1,0:T(8,128)(2,1)} %param.18) | copy-start | bytes 3538948
  7.2 25.5 %all-gather.6.cloned.1.call-start = ((), (), s32[]{:S(2)}) async-start(), calls=%async_computation.5 | async-start | bytes 1966080 | tf_op jit(solution)/shard_map/all_gather | solution.py:59
  9.1 2.6 copy-start.46
  11.8 73.2 %reduce-scatter.6.cloned.1.call-start = ((), (), s32[]{:S(2)}) async-start(), calls=%async_computation.6 | async-start | bytes 3932160 | tf_op jit(solution)/shard_map/reduce_scatter | solution.py:63
  14.2 23.0 %copy-start.9 = (f32[512,32]{0,1:T(8,128)}, f32[512,32]{0,1:T(8,128)S(1)}, u32[]{:S(2)}) copy-start(f32[512,32]{0,1:T(8,128)S(1)} %get-tuple-element.71) | copy-start | bytes 196612
  14.2 23.0 %copy-start.11 = (f32[512,32]{0,1:T(8,128)}, f32[512,32]{0,1:T(8,128)S(1)}, u32[]{:S(2)}) copy-start(f32[512,32]{0,1:T(8,128)S(1)} %get-tuple-element.72) | copy-start | bytes 196612
  15.8 21.5 %copy-start.6 = (pred[512,512]{0,1:T(8,128)(4,1)}, pred[512,512]{0,1:T(8,128)(4,1)S(1)}, u32[]{:S(2)}) copy-start(pred[512,512]{0,1:T(8,128)(4,1)S(1)} %compare_and_fusion) | copy-start | bytes 786436
  34.9 2.5 copy-start.31
  34.9 2.5 copy-start.33
  37.3 1.3 copy-start.25
  37.3 1.3 copy-start.27
  38.6 3.6 copy-start.1
  38.6 3.6 copy-start.38
  38.6 2.6 copy-start.2
  38.6 3.0 copy-start.17
  41.6 1.9 copy-start.39
  42.2 1.2 copy-start.29
  43.5 0.7 copy-start.23
  46.9 0.7 copy-start.48
  46.9 139.6 %all-gather.8.cloned.1.call-start = ((), (), s32[]{:S(2)}) async-start(), calls=%async_computation.7 | async-start | bytes 12976128 | tf_op jit(solution)/shard_map/all_gather | solution.py:67
  47.6 107.7 %copy-start.35 = (f32[1536]{0:T(1024)}, f32[1536]{0:T(1024)S(1)}, u32[]{:S(2)}) copy-start(f32[1536]{0:T(1024)S(1)} %convert_element_type.133) | copy-start | bytes 18436
  87.0 0.6 copy-start.44
  88.5 195.3 %all-gather.10.cloned.1.call-start = ((), (), s32[]{:S(2)}) async-start(), calls=%async_computation.9 | async-start | bytes 12976128 | tf_op jit(solution)/shard_map/all_gather | solution.py:67
  89.1 323.6 %reduce-scatter.12.cloned.1.call-start = ((), (), s32[]{:S(2)}) async-start(), calls=%async_computation.11 | async-start | bytes 270336 | tf_op jit(solution)/shard_map/reduce_scatter | solution.py:71
  186.5 10.3 copy-start.13
  186.5 10.3 copy-start.15
  298.8 356.9 %reduce-scatter.10.cloned.1.call-start = ((), (), s32[]{:S(2)}) async-start(), calls=%async_computation.10 | async-start | bytes 12976128 | tf_op jit(solution)/shard_map/reduce_scatter | solution.py:71
  300.1 0.6 copy-start.41
  463.4 7.4 copy-start.14
  463.4 7.3 copy-start.16
  470.8 10.4 copy-start.3
  496.5 321.1 %reduce-scatter.8.cloned.1.call-start = ((), (), s32[]{:S(2)}) async-start(), calls=%async_computation.8 | async-start | bytes 12976128 | tf_op jit(solution)/shard_map/reduce_scatter | solution.py:71
  506.3 333.5 %all-gather.12.cloned.1.call-start = ((), (), s32[]{:S(2)}) async-start(), calls=%async_computation.12 | async-start | bytes 1966080 | tf_op jit(solution)/shard_map/all_gather | solution.py:59
  820.5 21.7 %copy-start.7 = (pred[512,512]{0,1:T(8,128)(4,1)S(1)}, pred[512,512]{0,1:T(8,128)(4,1)}, u32[]{:S(2)}) copy-start(pred[512,512]{0,1:T(8,128)(4,1)} %copy-done.6) | copy-start | bytes 786436
  820.5 172.7 %all-reduce.8.cloned.1.call-start = ((), (), s32[]{:S(2)}) async-start(), calls=%async_computation.15 | async-start | bytes 6291456 | tf_op jit(solution)/shard_map/psum | solution.py:344
  839.8 6.5 slice-start
  842.2 4.1 slice-start.1
  842.2 4.1 copy-start.30
  850.9 4.7 copy-start.26
  850.9 4.7 copy-start.28
  855.5 1.1 copy-start.32
  855.6 1.1 copy-start.34
  855.6 1.8 copy-start.10
  855.6 1.8 copy-start.12
  856.7 1.0 copy-start.24
  856.7 1.5 copy-start.50
  864.1 2.4 copy-start.19
  864.1 170.0 %reduce-scatter.14.cloned.1.call-start = ((), (), s32[]{:S(2)}) async-start(), calls=%async_computation.13 | async-start | bytes 3932160 | tf_op jit(solution)/shard_map/reduce_scatter | solution.py:63
  866.5 1.0 copy-start.18
  869.7 292.9 %all-reduce.6.cloned.1.call-start = ((), (), s32[]{:S(2)}) async-start(), calls=%async_computation.14 | async-start | bytes 196608 | tf_op jit(solution)/shard_map/psum | solution.py:349
  888.7 3.1 copy-start.5
  888.7 3.1 copy-start.36
  888.7 3.1 copy-start.37
  888.7 3.1 copy-start.42
  888.7 3.1 copy-start.43
  888.7 3.1 copy-start.45
  993.2 4.1 copy-start.22
  993.2 5.8 copy-start.21
  997.3 36.8 %copy-start.4 = (bf16[128,1536]{1,0:T(8,128)(2,1)S(1)}, bf16[128,1536]{1,0:T(8,128)(2,1)}, u32[]{:S(2)}) copy-start(bf16[128,1536]{1,0:T(8,128)(2,1)} %param.16) | copy-start | bytes 1179652
  997.3 36.8 %copy-start.47 = (f32[128]{0:T(128)S(1)}, f32[128]{0:T(128)}, u32[]{:S(2)}) copy-start(f32[128]{0:T(128)} %copy-done.46) | copy-start | bytes 1540
  999.0 36.5 %copy-start.8 = (f32[128,1536]{1,0:T(8,128)S(1)}, f32[128,1536]{1,0:T(8,128)}, u32[]{:S(2)}) copy-start(f32[128,1536]{1,0:T(8,128)} %get-tuple-element.47) | copy-start | bytes 2359300
  999.0 36.5 %copy-start.49 = (f32[128]{0:T(128)S(1)}, f32[128]{0:T(128)}, u32[]{:S(2)}) copy-start(f32[128]{0:T(128)} %get-tuple-element.76) | copy-start | bytes 1540
  999.0 38.9 %copy-start.40 = (f32[1536]{0:T(1024)S(1)}, f32[1536]{0:T(1024)}, u32[]{:S(2)}) copy-start(f32[1536]{0:T(1024)} %get-tuple-element.36) | copy-start | bytes 18436
Sparse Core Ops, SparseCore 0:
  11.9 20.8 all-gather.5
  47.0 37.9 reduce-scatter.5
  88.9 97.5 all-gather.7
  189.6 94.2 all-gather.9
  299.0 113.6 reduce-scatter.11
  496.6 159.0 reduce-scatter.9
  662.8 154.7 reduce-scatter.7
  820.6 19.1 all-gather.11
  864.2 128.9 all-reduce.7
  995.8 38.2 reduce-scatter.13
  1040.3 122.3 all-reduce.5
where the time goes:
time: 1180 us; the launch traced here: 1170 us
  waiting for transfers between devices  807 us (68%)
  blocking collectives  136 us (12%)
  matrix products  135 us (11%)
  other arithmetic  53.1 us (4%)
  local copies, waits for them, and re-layouts  23.5 us (2%)
  between operations  15.4 us (1%)
    reduce_scatter x3, waiting for transfers between devices, total_all(): lax.psum_scatter(value_rows, ('ep', 'tp'), scatter_dimension=0, tiled=True)  418 us
    all_gather x2, waiting for transfers between devices, gather_all(): return lax.all_gather(value_rows, ('ep', 'tp'), axis=0, tiled=True)  106 us
    psum x1, waiting for transfers between devices, local(): lax.psum(grad_w_query.astype(jnp.bfloat16), 'ep').astype(jnp.float32)  90.6 us
    all_gather x2, blocking collectives, gather_all(): return lax.all_gather(value_rows, ('ep', 'tp'), axis=0, tiled=True)  86 us
    psum x1, waiting for transfers between devices, local(): lax.psum((grad_gain_attn, grad_gain_ffn, grad_router), ('ep', 'tp'))  85.3 us
    reduce_scatter x2, waiting for transfers between devices, group_totals(): return lax.psum_scatter(value_rows, 'tp', scatter_dimension=0, tiled=True)  70.9 us
    psum x1, blocking collectives, local(): lax.psum((grad_gain_attn, grad_gain_ffn, grad_router), ('ep', 'tp'))  39.4 us
    all_gather x2, waiting for transfers between devices, group_rows(): return lax.all_gather(value_rows, 'tp', axis=0, tiled=True)  35 us
  transfers between devices with their start and end apart: 11, of which 11 were waited for; matrix products, arithmetic and copies ran while one was open for 9% of the time, Pallas kernels for 0%

commit v1 on v0

--- a/solution.py
+++ b/solution.py
@@ -9,6 +9,11 @@
 EPSILON = 1e-06
 ROPE_BASE = 10000.0
 EXACT_PRECISION = lax.Precision.HIGHEST
+
+
+def one_after_other(x, one, other):
+    partial = lax.psum(x, one)
+    return lax.psum(partial, other)
 
 
 def rope_tables(position, head_width):
@@ -346,8 +351,8 @@
         lax.psum(grad_w_value.astype(jnp.bfloat16), "ep").astype(jnp.float32),
         lax.psum(grad_w_out.astype(jnp.bfloat16), "ep").astype(jnp.float32),
     )
-    grad_gain_attn, grad_gain_ffn, grad_router = lax.psum(
-        (grad_gain_attn, grad_gain_ffn, grad_router), ("ep", "tp")
+    grad_gain_attn, grad_gain_ffn, grad_router = one_after_other(
+        (grad_gain_attn, grad_gain_ffn, grad_router), "tp", "ep"
     )
     return (
         output_own,

time: 1180 us -> 1140 us (0.966)
  waiting for transfers between devices: 807 us -> 763 us
    psum x1 -> x2, waiting for transfers between devices: 85.3 us -> 24 us  [the longest x1 24 us: one_after_other(): return lax.psum(partial, other)]
    psum x1, waiting for transfers between devices: 90.6 us -> 111 us  [local(): lax.psum(grad_w_query.astype(jnp.bfloat16), 'ep').astype(jnp.float32)]
    psum x1 -> x2, blocking collectives: 39.4 us -> 44.6 us  [the longest x1 34.1 us: one_after_other(): return lax.psum(partial, other)]
  transfers between devices with their start and end apart: 11 -> 12, of which waited for: 11 -> 11; matrix products, arithmetic and copies ran while one was open for 9% -> 12% of each run, Pallas kernels for 0% -> 0%
where the time goes in v1:
time: 1140 us; the launch traced here: 1130 us
  waiting for transfers between devices  763 us (67%)
  blocking collectives  142 us (12%)
  matrix products  133 us (12%)
  other arithmetic  53 us (5%)
  local copies, waits for them, and re-layouts  22 us (2%)
  between operations  15.8 us (1%)
    reduce_scatter x3, waiting for transfers between devices, total_all(): lax.psum_scatter(value_rows, ('ep', 'tp'), scatter_dimension=0, tiled=True)  419 us
    psum x1, waiting for transfers between devices, local(): lax.psum(grad_w_query.astype(jnp.bfloat16), 'ep').astype(jnp.float32)  111 us
    all_gather x2, waiting for transfers between devices, gather_all(): return lax.all_gather(value_rows, ('ep', 'tp'), axis=0, tiled=True)  105 us
    all_gather x2, blocking collectives, gather_all(): return lax.all_gather(value_rows, ('ep', 'tp'), axis=0, tiled=True)  86.7 us
    reduce_scatter x2, waiting for transfers between devices, group_totals(): return lax.psum_scatter(value_rows, 'tp', scatter_dimension=0, tiled=True)  70.9 us
    psum x1, blocking collectives, one_after_other(): return lax.psum(partial, other)  34.1 us
    all_gather x2, waiting for transfers between devices, group_rows(): return lax.all_gather(value_rows, 'tp', axis=0, tiled=True)  33.1 us
    psum x1, waiting for transfers between devices, one_after_other(): return lax.psum(partial, other)  24 us
  transfers between devices with their start and end apart: 12, of which 11 were waited for; matrix products, arithmetic and copies ran while one was open for 12% of the time, Pallas kernels for 0%

profile of v1, /device:TPU:8, one launch (start us, length us, event | category | flops | bytes accessed | tf_op | source)
XLA Modules:
  0.0 1129.9 jit_solution(4868831586487369892)
XLA Ops:
  7.3 1.3 fusion.29
  9.8 1.9 fusion.31
  14.2 1.6 compare_and_fusion
  15.8 16.9 %all-gather.6.cloned.1.call-done = bf16[512,1536]{1,0:T(8,128)(2,1)} async-done(((bf16[128,1536]{1,0:T(8,128)(2,1)}), bf16[512,1536]{1,0:T(8,128)(2,1)}) %all-gather.6.cloned.1.call-update) | async-done | bytes 1572880 | tf_op jit(solution)/shard_map/all_gather | solution.py:64
  32.7 2.1 fusion.66
  34.9 2.3 fusion.67
  39.5 1.7 copy-done.2
  44.2 2.6 fusion.68
  47.5 37.4 %reduce-scatter.6.cloned.1.call-done = f32[128,1536]{1,0:T(8,128)} async-done(((f32[512,1536]{1,0:T(8,128)}), f32[128,1536]{1,0:T(8,128)}) %reduce-scatter.6.cloned.1.call-update) | async-done | bytes 786448 | tf_op jit(solution)/shard_map/reduce_scatter | solution.py:68
  84.9 1.4 multiply_reduce_fusion.2
  89.0 1.4 select_reduce_fusion
  90.4 1.6 copy.39
  93.9 1.4 convert_reduce_fusion.1
  95.8 1.3 dynamic-update-slice
  97.0 11.0 all-reduce
  108.1 1.3 reshape.451
  110.9 4.3 convert_reduce_fusion
  115.2 1.4 fusion.63
  116.5 37.3 %all_gather.30 = f32[4096,16]{0,1:T(8,128)} all-gather(f32[128,16]{0,1:T(8,128)S(1)} %get-tuple-element.50), channel_id=1, replica_groups=mesh['ep'=8,'tp'=4] {'ep','tp'}, dimensions={0}, use_global_device_ids=true | all-gather | bytes 270336 | tf_op jit(solution)/shard_map/all_gather | solution.py:72
  153.8 2.1 slice_bitcast_fusion.3
  155.9 2.0 slice_bitcast_fusion.1
  157.9 28.3 %all-gather.8.cloned.1.call-done = bf16[4096,1536]{1,0:T(8,128)(2,1)} async-done(((bf16[128,1536]{1,0:T(8,128)(2,1)}), bf16[4096,1536]{1,0:T(8,128)(2,1)}) %all-gather.8.cloned.1.call-update) | async-done | bytes 12582928 | tf_op jit(solution)/shard_map/all_gather | solution.py:72
  186.2 10.3 fusion.38
  196.5 10.2 fusion.40
  206.7 76.8 %all-gather.10.cloned.1.call-done = bf16[4096,1536]{1,0:T(8,128)(2,1)} async-done(((bf16[128,1536]{1,0:T(8,128)(2,1)}), bf16[4096,1536]{1,0:T(8,128)(2,1)}) %all-gather.10.cloned.1.call-update) | async-done | bytes 12582928 | tf_op jit(solution)/shard_map/all_gather | solution.py:72
  283.5 12.7 %bitcast_reduce_fusion = (f32[4096,2]{0,1:T(2,128)S(1)}, f32[4096,256]{0,1:T(8,128)}) fusion(f32[4096,256]{0,1:T(8,128)} %fusion.38, f32[4096,256]{0,1:T(8,128)} %fusion.40, bf16[4096,1536]{1,0:T(8,128)(2,1)} %all-gather.10.cloned.1.call-done, bf16[256,1536]{1,0:T(8,128)(2,1)} %bitcast.149), kind=kOutput, calls=%fused_computation.19 | convolution fusion | flops 3228557312 | bytes 25985024 | tf_op jit(solution)/shard_map/rd,fd->rf/dot_general | solution.py:253
  296.9 1.5 multiply_dynamic-update-slice_fusion
  301.6 110.7 %reduce-scatter.12.cloned.1.call-done = f32[128,16]{0,1:T(8,128)} async-done(((f32[4096,16]{0,1:T(8,128)}), f32[128,16]{0,1:T(8,128)}) %reduce-scatter.12.cloned.1.call-update) | async-done | bytes 8208 | tf_op jit(solution)/shard_map/reduce_scatter | solution.py:76
  413.6 49.4 %all_gather.27 = f32[4096,16]{0,1:T(8,128)S(1)} all-gather(f32[128,16]{0,1:T(8,128)S(1)} %get-tuple-element.72), channel_id=1, replica_groups=mesh['ep'=8,'tp'=4] {'ep','tp'}, dimensions={0}, use_global_device_ids=true | all-gather | bytes 270336 | tf_op jit(solution)/shard_map/all_gather | solution.py:72
  463.0 7.3 multiply_convert_fusion
  470.4 10.4 fusion.39
  480.8 15.4 %add_convert_fusion = bf16[4096,1536]{1,0:T(8,128)(2,1)} fusion(f32[4096,1536]{1,0:T(8,128)} %fusion.39, bf16[4096,256]{0,1:T(8,128)(2,1)} %get-tuple-element.55, bf16[1536,128]{1,0:T(8,128)(2,1)} %get-tuple-element.66, bf16[1536,128]{1,0:T(8,128)(2,1)} %get-tuple-element.65), kind=kOutput, calls=%fused_computation | convolution fusion | flops 3235381248 | bytes 40632320 | tf_op jit(solution)/shard_map/rf,df->rd/dot_general | solution.py:265
  496.3 9.8 convolution_convert_fusion
  506.1 149.7 %reduce-scatter.10.cloned.1.call-done = bf16[128,1536]{1,0:T(8,128)(2,1)} async-done(((bf16[4096,1536]{1,0:T(8,128)(2,1)}), bf16[128,1536]{1,0:T(8,128)(2,1)}) %reduce-scatter.10.cloned.1.call-update) | async-done | bytes 393232 | tf_op jit(solution)/shard_map/reduce_scatter | solution.py:76
  655.8 3.3 multiply_reduce_fusion
  659.6 158.1 %reduce-scatter.8.cloned.1.call-done = bf16[128,1536]{1,0:T(8,128)(2,1)} async-done(((bf16[4096,1536]{1,0:T(8,128)(2,1)}), bf16[128,1536]{1,0:T(8,128)(2,1)}) %reduce-scatter.8.cloned.1.call-update) | async-done | bytes 393232 | tf_op jit(solution)/shard_map/reduce_scatter | solution.py:76
  817.7 2.9 fusion.62
  821.4 2.0 fusion.44
  823.7 16.2 %all-gather.12.cloned.1.call-done = bf16[512,1536]{1,0:T(8,128)(2,1)} async-done(((bf16[128,1536]{1,0:T(8,128)(2,1)}), bf16[512,1536]{1,0:T(8,128)(2,1)}) %all-gather.12.cloned.1.call-update) | async-done | bytes 1572880 | tf_op jit(solution)/shard_map/all_gather | solution.py:64
  839.9 2.4 convolution_convert_fusion.5
  842.3 4.1 fusion.26
  846.5 4.5 fusion.4
  851.0 4.7 fusion.6
  858.4 1.8 convolution_convert_fusion.1
  861.3 1.8 convolution_convert_fusion.2
  864.3 2.3 fusion.69
  867.7 2.2 convolution_add_fusion
  870.2 7.0 fusion.17
  877.3 1.6 copy.44
  878.9 7.0 fusion.14
  885.9 1.6 copy.43
  887.5 9.8 fusion.70
  897.4 110.6 %all-reduce.12.cloned.1.call-done = (bf16[384,1536]{1,0:T(8,128)(2,1)}, bf16[128,1536]{1,0:T(8,128)(2,1)}, bf16[128,1536]{1,0:T(8,128)(2,1)}, bf16[384,1536]{1,0:T(8,128)(2,1)}) async-done(((bf16[384,1536]{1,0:T(8,128)(2,1)}, bf16[128,1536]{1,0:T(8,128)(2,1)}, bf16[128,1536]{1,0:T(8,128)(2,1)}, bf16[384,1536]{1,0:T(8,128)(2,1)}), (bf16[384,1536]{1,0:T(8,128)(2,1)}, bf16[128,1536]{1,0:T(8,128)(2,1)}, ...) | async-done | bytes 3145744 | tf_op jit(solution)/shard_map/psum | solution.py:349
  1008.0 2.1 convert_element_type.156
  1010.1 2.0 convert_element_type.158
  1012.0 1.7 convert_element_type.154
  1013.7 1.7 convert_element_type.160
  1015.4 33.4 %reduce-scatter.14.cloned.1.call-done = f32[128,1536]{1,0:T(8,128)} async-done(((f32[512,1536]{1,0:T(8,128)}), f32[128,1536]{1,0:T(8,128)}) %reduce-scatter.14.cloned.1.call-update) | async-done | bytes 786448 | tf_op jit(solution)/shard_map/reduce_scatter | solution.py:68
  1048.8 1.4 fusion.37
  1050.2 2.4 fusion.34
  1052.6 10.5 all-reduce.2
  1063.1 34.1 %all-reduce.1 = (f32[1536]{0:T(1024)}, f32[1536]{0:T(1024)}) all-reduce(f32[1536]{0:T(1024)S(1)} %get-tuple-element.42, f32[1536]{0:T(1024)S(1)} %get-tuple-element.43), channel_id=1, replica_groups=mesh['ep'=8,'tp'=4] {'ep'}, use_global_device_ids=true, to_apply=%region_22.23 | all-reduce | flops 3072 | bytes 24576 | tf_op jit(solution)/shard_map/psum | solution.py:16
  1097.2 24.0 %all-reduce.10.cloned.1.call-done = f32[16,1536]{1,0:T(8,128)} async-done(((f32[16,1536]{1,0:T(8,128)}), f32[16,1536]{1,0:T(8,128)}) %all-reduce.10.cloned.1.call-update) | async-done | bytes 98320 | tf_op jit(solution)/shard_map/psum | solution.py:16
  1121.2 1.5 copy.61
  (157 shorter events, 28.5 us)
Async XLA Ops:
  7.2 37.0 %copy-start = (bf16[384,1536]{1,0:T(8,128)(2,1)S(1)}, bf16[384,1536]{1,0:T(8,128)(2,1)}, u32[]{:S(2)}) copy-start(bf16[384,1536]{1,0:T(8,128)(2,1)} %param.21) | copy-start | bytes 3538948
  7.2 27.6 %copy-start.19 = (bf16[384,1536]{1,0:T(8,128)(2,1)S(1)}, bf16[384,1536]{1,0:T(8,128)(2,1)}, u32[]{:S(2)}) copy-start(bf16[384,1536]{1,0:T(8,128)(2,1)} %param.18) | copy-start | bytes 3538948
  7.2 25.5 %all-gather.6.cloned.1.call-start = ((), (), s32[]{:S(2)}) async-start(), calls=%async_computation.5 | async-start | bytes 1966080 | tf_op jit(solution)/shard_map/all_gather | solution.py:64
  9.1 2.6 copy-start.40
  11.7 73.2 %reduce-scatter.6.cloned.1.call-start = ((), (), s32[]{:S(2)}) async-start(), calls=%async_computation.6 | async-start | bytes 3932160 | tf_op jit(solution)/shard_map/reduce_scatter | solution.py:68
  14.1 23.0 %copy-start.8 = (f32[512,32]{0,1:T(8,128)}, f32[512,32]{0,1:T(8,128)S(1)}, u32[]{:S(2)}) copy-start(f32[512,32]{0,1:T(8,128)S(1)} %get-tuple-element.73) | copy-start | bytes 196612
  14.2 23.0 %copy-start.10 = (f32[512,32]{0,1:T(8,128)}, f32[512,32]{0,1:T(8,128)S(1)}, u32[]{:S(2)}) copy-start(f32[512,32]{0,1:T(8,128)S(1)} %get-tuple-element.74) | copy-start | bytes 196612
  15.8 21.5 %copy-start.5 = (pred[512,512]{0,1:T(8,128)(4,1)}, pred[512,512]{0,1:T(8,128)(4,1)S(1)}, u32[]{:S(2)}) copy-start(pred[512,512]{0,1:T(8,128)(4,1)S(1)} %compare_and_fusion) | copy-start | bytes 786436
  34.8 2.5 copy-start.30
  34.8 2.5 copy-start.32
  37.3 1.3 copy-start.24
  37.3 1.3 copy-start.26
  38.5 3.6 copy-start.1
  38.6 3.6 copy-start.35
  38.6 2.6 copy-start.2
  38.6 3.0 copy-start.16
  41.5 1.9 copy-start.36
  42.2 1.2 copy-start.28
  43.4 0.7 copy-start.22
  46.8 0.7 copy-start.42
  46.8 139.4 %all-gather.8.cloned.1.call-start = ((), (), s32[]{:S(2)}) async-start(), calls=%async_computation.7 | async-start | bytes 12976128 | tf_op jit(solution)/shard_map/all_gather | solution.py:72
  47.5 108.4 %copy-start.34 = (f32[1536]{0:T(1024)}, f32[1536]{0:T(1024)S(1)}, u32[]{:S(2)}) copy-start(f32[1536]{0:T(1024)S(1)} %convert_element_type.133) | copy-start | bytes 18436
  86.9 0.6 copy-start.39
  88.4 195.1 %all-gather.10.cloned.1.call-start = ((), (), s32[]{:S(2)}) async-start(), calls=%async_computation.9 | async-start | bytes 12976128 | tf_op jit(solution)/shard_map/all_gather | solution.py:72
  88.9 323.4 %reduce-scatter.12.cloned.1.call-start = ((), (), s32[]{:S(2)}) async-start(), calls=%async_computation.11 | async-start | bytes 270336 | tf_op jit(solution)/shard_map/reduce_scatter | solution.py:76
  186.2 10.3 copy-start.12
  186.2 10.3 copy-start.14
  298.5 357.3 %reduce-scatter.10.cloned.1.call-start = ((), (), s32[]{:S(2)}) async-start(), calls=%async_computation.10 | async-start | bytes 12976128 | tf_op jit(solution)/shard_map/reduce_scatter | solution.py:76
  299.8 0.6 copy-start.38
  463.0 7.4 copy-start.13
  463.0 7.3 copy-start.15
  470.4 10.4 copy-start.3
  496.3 321.5 %reduce-scatter.8.cloned.1.call-start = ((), (), s32[]{:S(2)}) async-start(), calls=%async_computation.8 | async-start | bytes 12976128 | tf_op jit(solution)/shard_map/reduce_scatter | solution.py:76
  506.1 333.8 %all-gather.12.cloned.1.call-start = ((), (), s32[]{:S(2)}) async-start(), calls=%async_computation.12 | async-start | bytes 1966080 | tf_op jit(solution)/shard_map/all_gather | solution.py:64
  820.6 76.7 %all-reduce.8.cloned.1.call-start = ((), (), s32[]{:S(2)}) async-start(), calls=%async_computation.14 | async-start | bytes 196608 | tf_op jit(solution)/shard_map/psum | solution.py:15
  823.4 18.9 %copy-start.6 = (pred[512,512]{0,1:T(8,128)(4,1)S(1)}, pred[512,512]{0,1:T(8,128)(4,1)}, u32[]{:S(2)}) copy-start(pred[512,512]{0,1:T(8,128)(4,1)} %copy-done.5) | copy-start | bytes 786436
  823.4 184.5 %all-reduce.12.cloned.1.call-start = ((), (), s32[]{:S(2)}) async-start(), calls=%async_computation.16 | async-start | bytes 6291456 | tf_op jit(solution)/shard_map/psum | solution.py:349
  839.9 6.5 slice-start
  842.3 4.1 slice-start.1
  842.3 4.1 copy-start.29
  851.0 4.7 copy-start.25
  851.0 4.7 copy-start.27
  855.7 1.1 copy-start.31
  855.7 1.1 copy-start.33
  855.7 1.8 copy-start.9
  855.7 1.8 copy-start.11
  856.8 1.0 copy-start.23
  856.8 1.5 copy-start.44
  864.3 2.4 copy-start.18
  864.3 184.6 %reduce-scatter.14.cloned.1.call-start = ((), (), s32[]{:S(2)}) async-start(), calls=%async_computation.13 | async-start | bytes 3932160 | tf_op jit(solution)/shard_map/reduce_scatter | solution.py:68
  866.7 1.0 copy-start.17
  869.9 251.3 %all-reduce.10.cloned.1.call-start = ((), (), s32[]{:S(2)}) async-start(), calls=%async_computation.15 | async-start | bytes 196608 | tf_op jit(solution)/shard_map/psum | solution.py:16
  1008.0 4.1 copy-start.21
  1008.0 5.8 copy-start.20
  1012.0 36.8 %copy-start.4 = (bf16[128,1536]{1,0:T(8,128)(2,1)S(1)}, bf16[128,1536]{1,0:T(8,128)(2,1)}, u32[]{:S(2)}) copy-start(bf16[128,1536]{1,0:T(8,128)(2,1)} %param.16) | copy-start | bytes 1179652
  1012.0 36.8 %copy-start.41 = (f32[128]{0:T(128)S(1)}, f32[128]{0:T(128)}, u32[]{:S(2)}) copy-start(f32[128]{0:T(128)} %copy-done.40) | copy-start | bytes 1540
  1013.7 36.5 %copy-start.7 = (f32[128,1536]{1,0:T(8,128)S(1)}, f32[128,1536]{1,0:T(8,128)}, u32[]{:S(2)}) copy-start(f32[128,1536]{1,0:T(8,128)} %get-tuple-element.49) | copy-start | bytes 2359300
  1013.7 36.5 %copy-start.43 = (f32[128]{0:T(128)S(1)}, f32[128]{0:T(128)}, u32[]{:S(2)}) copy-start(f32[128]{0:T(128)} %get-tuple-element.78) | copy-start | bytes 1540
  1013.7 38.9 %copy-start.37 = (f32[1536]{0:T(1024)S(1)}, f32[1536]{0:T(1024)}, u32[]{:S(2)}) copy-start(f32[1536]{0:T(1024)} %get-tuple-element.36) | copy-start | bytes 18436
Sparse Core Ops, SparseCore 0:
  11.8 20.8 all-gather.5
  47.0 37.9 reduce-scatter.5
  88.8 97.3 all-gather.7
  189.3 94.1 all-gather.9
  298.6 113.6 reduce-scatter.11
  496.4 159.3 reduce-scatter.9
  662.9 154.8 reduce-scatter.7
  820.8 19.1 all-gather.11
  842.8 31.3 all-reduce.7
  879.0 128.9 all-reduce.11
  1010.5 38.2 reduce-scatter.13
  1052.4 68.7 all-reduce.9
